TPU v7x, 32 devices: a whole 2x2x4 slice. The times are simulated.
32 devices in a mesh: grp: 2 (over x), blk: 16 (over z, y, core).
Axes of the slice: x: 2, y: 2, z: 4, core: 2. Of those that a mesh axis runs over, the one named last changes fastest.
Arguments:
- queries: bfloat16 [32, 5120], P(('grp', 'blk')), parts along dimension 0, may hold values from -128 to 128
- home_device: int32 [8], P('grp'), parts along dimension 0, may hold values from 0 to 15, as said below
- lengths: int32 [8], P('grp'), parts along dimension 0, may hold values from 256 to 2048, as said below
- key_cache: bfloat16 [8, 2048, 1024], P('grp', 'blk'), parts along dimension 0, may hold values from -8 to 8
- value_cache: bfloat16 [8, 2048, 1024], P('grp', 'blk'), parts along dimension 0, may hold values from -6 to 6
- residual: bfloat16 [8, 5120], P('grp', 'blk'), parts along dimension 0, may hold values from -4 to 4
- out_weight: bfloat16 [5120, 5120], P('blk'), may hold values from -0.125 to 0.125
- ffn_gain: float32 [5120], replicated, may hold values from 0.5 to 1.5
- gate_weight: bfloat16 [5120, 27648], P(None, 'blk'), may hold values from -0.078125 to 0.078125
- up_weight: bfloat16 [5120, 27648], P(None, 'blk'), may hold values from -0.078125 to 0.078125
- down_weight: bfloat16 [27648, 5120], P('blk'), may hold values from -0.0546875 to 0.0546875
- query_gain: float32 [5120], replicated, may hold values from 0.5 to 1.5
- query_weight: bfloat16 [5120, 5120], P(None, 'blk'), may hold values from -0.078125 to 0.078125
- query_bias: float32 [5120], P('blk'), may hold values from -3 to 3
Outputs:
- hidden_out: bfloat16 [8, 5120], P('grp', 'blk'), parts along dimension 0
- next_queries: bfloat16 [32, 5120], P(('grp', 'blk')), parts along dimension 0
There are 2 independent parts, one for each index of `grp`. A program takes and returns all parts, laid end to end along the dimension named above; an argument that names none is the same for every part. Nothing has to cross between parts.
Inputs may be any that keep to these rules, and one draw needn't show every extreme that they name: `home_device`: distinct device indices below 16; the last device is home to one sequence in every draw; rows of queries at devices that are home to no sequence are not read. `lengths`: one sequence of every draw has the full 2048 positions.
All inputs are finite; a program needn't handle non-finite values.
Results may differ from a plain program's by a relative error of at most 0.018.
Values may be sent and summed in bfloat16 or wider, within the bound.
A program may use at most 128 MiB of HBM per device.

v0:
```python
import jax
import jax.numpy as jnp
from jax import lax
from jax.sharding import PartitionSpec as P

HQ = 40
KVH = 8
HEAD = 128


def combined_all(value, axis, combine):
    everything = jax.tree.map(lambda part: lax.all_gather(part, axis), value)
    first = jax.tree.map(lambda part: part[0], everything)

    def step(k, so_far):
        return combine(so_far, jax.tree.map(lambda part: part[k], everything))

    return lax.fori_loop(1, lax.axis_size(axis), step, first)


def rms_scale(carried, gain_row):
    widened = carried.astype(jnp.float32)
    spread = jnp.mean(widened * widened, axis=-1, keepdims=True)
    return (widened * lax.rsqrt(spread + 1e-06) * gain_row).astype(jnp.bfloat16)


def merge_parts(former, latter):
    peak_former, total_former, sum_former = former
    peak_latter, total_latter, sum_latter = latter
    highest = jnp.maximum(peak_former, peak_latter)
    scale_former = jnp.exp(peak_former - highest)
    scale_latter = jnp.exp(peak_latter - highest)
    merged_total = total_former * scale_former + total_latter * scale_latter
    merged_sum = sum_former * scale_former[..., None] + sum_latter * scale_latter[..., None]
    return (highest, merged_total, merged_sum)


def branch_parts(partial_sum):
    return lax.psum_scatter(partial_sum, "blk", scatter_dimension=1, tiled=True)


def spread_rows(shard_rows):
    return lax.all_gather(shard_rows, "blk", axis=1, tiled=True)


def local(
    queries,
    home_device,
    lengths,
    key_cache,
    value_cache,
    residual,
    out_weight,
    ffn_gain,
    gate_weight,
    up_weight,
    down_weight,
    query_gain,
    query_weight,
    query_bias,
):
    shard_count = lax.axis_size("blk")
    my_index = lax.axis_index("blk")
    seq_count = home_device.shape[0]
    feat_width = residual.shape[1]
    model_width = queries.shape[1]
    group_size = HQ // KVH
    cache_span = key_cache.shape[1]
    home_pick = (home_device[:, None] == jnp.arange(shard_count, dtype=jnp.int32)[None, :]).astype(
        jnp.bfloat16
    )
    every_row = lax.all_gather(queries, "blk", axis=0, tiled=True)
    seq_rows = jnp.dot(home_pick, every_row, preferred_element_type=jnp.float32).astype(
        jnp.bfloat16
    )
    positions = my_index * cache_span + jnp.arange(cache_span, dtype=jnp.int32)
    usable = positions[None, :] < lengths[:, None]
    query_heads = seq_rows.reshape(seq_count, KVH, group_size, HEAD)
    key_heads = key_cache.reshape(seq_count, cache_span, KVH, HEAD)
    value_heads = value_cache.reshape(seq_count, cache_span, KVH, HEAD)
    scores = jnp.einsum(
        "skgd,stkd->skgt", query_heads, key_heads, preferred_element_type=jnp.float32
    ) * HEAD ** (-0.5)
    allowed = usable[:, None, None, :]
    masked = jnp.where(allowed, scores, -1e30)
    local_peak = jnp.max(masked, axis=-1)
    raised = jnp.where(allowed, jnp.exp(masked - local_peak[..., None]), 0.0)
    local_total = jnp.sum(raised, axis=-1)
    local_sum = jnp.einsum(
        "skgt,stkd->skgd",
        raised.astype(jnp.bfloat16),
        value_heads,
        preferred_element_type=jnp.float32,
    )
    global_peak, global_total, summed = combined_all(
        (local_peak, local_total, local_sum), "blk", merge_parts
    )
    context = (
        (summed / global_total[..., None]).reshape(seq_count, model_width).astype(jnp.bfloat16)
    )
    context_mine = lax.dynamic_slice_in_dim(context, my_index * feat_width, feat_width, 1)
    attn_partial = jnp.dot(context_mine, out_weight, preferred_element_type=jnp.float32)
    carried_mine = (residual.astype(jnp.float32) + branch_parts(attn_partial)).astype(jnp.bfloat16)
    carried_full = spread_rows(carried_mine)
    ffn_input = rms_scale(carried_full, ffn_gain)
    gate_part = jnp.dot(ffn_input, gate_weight, preferred_element_type=jnp.float32)
    up_part = jnp.dot(ffn_input, up_weight, preferred_element_type=jnp.float32)
    activated = (jax.nn.silu(gate_part) * up_part).astype(jnp.bfloat16)
    ffn_partial = jnp.dot(activated, down_weight, preferred_element_type=jnp.float32)
    hidden_mine = (carried_mine.astype(jnp.float32) + branch_parts(ffn_partial)).astype(
        jnp.bfloat16
    )
    hidden_full = spread_rows(hidden_mine)
    query_input = rms_scale(hidden_full, query_gain)
    fresh_query = (
        jnp.dot(query_input, query_weight, preferred_element_type=jnp.float32) + query_bias
    ).astype(jnp.bfloat16)
    outgoing = jnp.dot(home_pick.T, fresh_query, preferred_element_type=jnp.float32).astype(
        jnp.bfloat16
    )
    next_rows = lax.all_to_all(outgoing, "blk", split_axis=0, concat_axis=1, tiled=True)
    return (hidden_mine, next_rows)


def solution(mesh):
    placed = (
        P(("grp", "blk"), None),
        P("grp"),
        P("grp"),
        P("grp", "blk", None),
        P("grp", "blk", None),
        P("grp", "blk"),
        P("blk", None),
        P(),
        P(None, "blk"),
        P(None, "blk"),
        P("blk", None),
        P(),
        P(None, "blk"),
        P("blk"),
    )
    return jax.shard_map(
        local,
        mesh=mesh,
        in_specs=placed,
        out_specs=(P("grp", "blk"), P(("grp", "blk"), None)),
        check_vma=False,
    )
```

profile of v0, /device:TPU:0, one launch (start us, length us, event | category | flops | bytes accessed | tf_op | source)
XLA Modules:
  0.0 329.2 jit_solution(3780745455840544144)
XLA Ops:
  7.2 24.4 %all-gather.3 = bf16[16,1,5120]{2,1,0:T(2,128)(2,1)S(1)} all-gather(bf16[1,1,5120]{2,1,0:T(2,128)(2,1)} %bitcast.74), channel_id=1, replica_groups=mesh['grp'=2,'blk'=16] {'blk'}, dimensions={0}, use_global_device_ids=true | all-gather | bytes 174080 | tf_op jit(solution)/shard_map/all_gather | solution.py:72
  31.6 0.9 convolution_convert_fusion
  33.3 1.9 fusion.39
  35.2 1.7 fusion.8
  37.9 18.2 %all-gather.1 = f32[64,8,5]{2,1,0:T(8,128)S(1)} all-gather(f32[4,8,5]{2,1,0:T(8,128)S(1)} %fusion.16), channel_id=3, replica_groups=mesh['grp'=2,'blk'=16] {'blk'}, dimensions={0}, use_global_device_ids=true | all-gather | bytes 10880 | tf_op jit(solution)/shard_map/all_gather | solution.py:12
  56.7 1.1 copy.77
  57.8 0.8 copy.74
  58.6 19.7 %all-gather = f32[64,8,5]{2,1,0:T(8,128)S(1)} all-gather(f32[4,8,5]{2,1,0:T(8,128)} %copy-done.2), channel_id=2, replica_groups=mesh['grp'=2,'blk'=16] {'blk'}, dimensions={0}, use_global_device_ids=true | all-gather | bytes 10880 | tf_op jit(solution)/shard_map/all_gather | solution.py:12
  78.9 1.1 copy.76
  80.0 0.8 copy.73
  80.8 0.9 slice.17
  81.8 30.4 %while.19 = (s32[]{:T(128)}, f32[4,8,5]{1,0,2:T(4,128)S(1)}, f32[4,8,5]{1,0,2:T(4,128)S(1)}, f32[4,8,5,128]{3,2,1,0:T(8,128)S(1)}, f32[16,4,8,5]{2,1,3,0:T(4,128...) while((s32[]{:T(128)}, f32[4,8,5]{1,0,2:T(4,128)S(1)}, ...), condition=%wide.region_3.4_spmd, body=%wide.region_2.3_spmd.sunk | while | flops 62405 | bytes 418711 | solution.py:18
  81.8 0.8 fusion.50
  82.7 0.9 constant_dynamic-slice_fusion.2
  83.8 0.8 fusion.50
  84.7 0.9 constant_dynamic-slice_fusion.2
  86.8 0.9 constant_dynamic-slice_fusion.2
  88.8 0.9 constant_dynamic-slice_fusion.2
  89.9 0.8 fusion.50
  90.8 0.9 constant_dynamic-slice_fusion.2
  91.9 0.8 fusion.50
  92.9 0.9 constant_dynamic-slice_fusion.2
  94.9 0.9 constant_dynamic-slice_fusion.2
  96.0 0.8 fusion.50
  96.9 0.9 constant_dynamic-slice_fusion.2
  98.0 0.8 fusion.50
  98.9 0.9 constant_dynamic-slice_fusion.2
  100.0 0.8 fusion.50
  101.0 0.9 constant_dynamic-slice_fusion.2
  103.0 0.9 constant_dynamic-slice_fusion.2
  104.1 0.8 fusion.50
  105.0 0.9 constant_dynamic-slice_fusion.2
  106.1 0.8 fusion.50
  107.1 0.9 constant_dynamic-slice_fusion.2
  108.1 0.8 fusion.50
  109.1 0.9 constant_dynamic-slice_fusion.2
  111.1 0.9 constant_dynamic-slice_fusion.2
  112.5 3.2 convolution_bitcast_fusion
  115.7 61.8 %reduce-scatter.7.cloned.1.call-done = f32[320,4]{1,0:T(8,128)} async-done(((f32[5120,4]{1,0:T(8,128)}), f32[320,4]{1,0:T(8,128)}) %reduce-scatter.7.cloned.1.call-update) | async-done | bytes 5136
  177.5 1.0 copy.88
  178.5 19.3 %all-gather.4 = bf16[16,320,4]{1,2,0:T(4,128)(2,1)S(1)} all-gather(bf16[1,320,4]{1,2,0:T(4,128)(2,1)S(1)} %fusion.36), channel_id=1, replica_groups=mesh['grp'=2,'blk'=16] {'blk'}, dimensions={0}, use_global_device_ids=true | all-gather | bytes 43520 | tf_op jit(solution)/shard_map/all_gather | solution.py:43
  198.1 10.7 %fusion.37 = f32[4,1728]{1,0:T(4,128)S(1)} fusion(bf16[5120,1728]{0,1:T(8,128)(2,1)} %param.24, f32[5120,4]{0,1:T(4,128)S(1)} %reshape.90, f32[5120]{0:T(1024)S(1)} %copy-done.3, f32[4]{0:T(128)S(1)} %add_rsqrt_fusion.1), kind=kOutput, calls=%fused_computation.63 | convolution fusion | flops 70840320 | bytes 17824784 | tf_op jit(solution)/shard_map/dot_general | solution.py:106
  208.8 17.3 %convolution_bitcast_fusion.1 = f32[5120,4]{1,0:T(8,128)} fusion(bf16[1728,5120]{1,0:T(8,128)(2,1)} %param.26, bf16[5120,1728]{0,1:T(8,128)(2,1)} %param.25, f32[4,1728]{1,0:T(4,128)S(1)} %fusion.37, f32[5120,4]{0,1:T(4,128)S(1)} %reshape.90, f32[5120]{0:T(1024)S(1)} %copy-done.3, f32[4]{0:T(128)S(1)} %add_rsqrt_fusion.1), kind=kOutput, calls=%fused_computation.11 | convolution fusion | flops 141660672 | bytes 35601424
  226.1 61.6 %reduce-scatter.9.cloned.1.call-done = f32[320,4]{1,0:T(8,128)} async-done(((f32[5120,4]{1,0:T(8,128)}), f32[320,4]{1,0:T(8,128)}) %reduce-scatter.9.cloned.1.call-update) | async-done | bytes 5136
  287.7 1.0 copy.90
  288.8 19.3 %all-gather.5 = bf16[16,320,4]{1,2,0:T(4,128)(2,1)S(1)} all-gather(bf16[1,320,4]{1,2,0:T(4,128)(2,1)S(1)} %bitcast.75), channel_id=1, replica_groups=mesh['grp'=2,'blk'=16] {'blk'}, dimensions={0}, use_global_device_ids=true | all-gather | bytes 43520 | tf_op jit(solution)/shard_map/all_gather | solution.py:43
  308.4 3.0 fusion.6
  312.7 9.1 %all_to_all.16 = bf16[16,2,160]{2,1,0:T(2,128)(2,1)S(1)} all-to-all(bf16[16,2,160]{2,1,0:T(2,128)(2,1)S(1)} %reshape.97), channel_id=1, replica_groups=mesh['grp'=2,'blk'=16] {'blk'}, dimensions={0} | all-to-all | bytes 20480 | tf_op jit(solution)/shard_map/all_to_all | solution.py:121
  (102 shorter events, 15.2 us)
Async XLA Ops:
  7.2 105.3 %copy-start = (bf16[320,5120]{1,0:T(8,128)(2,1)S(1)}, bf16[320,5120]{1,0:T(8,128)(2,1)}, u32[]{:S(2)}) copy-start(bf16[320,5120]{1,0:T(8,128)(2,1)} %param.22) | copy-start | bytes 9830404
  7.2 73.6 %all-gather.8.cloned.1.call-start = ((), (), s32[]{:S(2)}) async-start(), calls=%async_computation.3 | async-start | bytes 1392640 | tf_op jit(solution)/shard_map/all_gather | solution.py:12
  35.2 2.4 copy-start.2
  37.6 139.9 %reduce-scatter.7.cloned.1.call-start = ((), (), s32[]{:S(2)}) async-start(), calls=%async_computation.4 | async-start | bytes 2785280
  112.4 66.0 %copy-start.6 = (bf16[4,320]{1,0:T(4,128)(2,1)S(1)}, bf16[4,320]{1,0:T(4,128)(2,1)}, u32[]{:S(2)}) copy-start(bf16[4,320]{1,0:T(4,128)(2,1)} %param.21) | copy-start | bytes 7684
  112.5 85.7 %copy-start.3 = (f32[5120]{0:T(1024)S(1)}, f32[5120]{0:T(1024)}, u32[]{:S(2)}) copy-start(f32[5120]{0:T(1024)} %param.23) | copy-start | bytes 61444
  115.7 172.1 %reduce-scatter.9.cloned.1.call-start = ((), (), s32[]{:S(2)}) async-start(), calls=%async_computation.5 | async-start | bytes 2785280
  226.1 82.3 %copy-start.4 = (f32[5120]{0:T(1024)S(1)}, f32[5120]{0:T(1024)}, u32[]{:S(2)}) copy-start(f32[5120]{0:T(1024)} %param.27) | copy-start | bytes 61444
  226.1 82.3 %copy-start.7 = (f32[320]{0:T(512)S(1)}, f32[320]{0:T(512)}, u32[]{:S(2)}) copy-start(f32[320]{0:T(512)} %param.29) | copy-start | bytes 3844
  226.1 82.3 %copy-start.8 = (s32[4]{0:T(128)S(1)}, s32[4]{0:T(128)}, u32[]{:S(2)}) copy-start(s32[4]{0:T(128)} %param.17) | copy-start | bytes 52
  226.1 96.6 %copy-start.1 = (bf16[320,5120]{1,0:T(8,128)(2,1)S(1)}, bf16[320,5120]{1,0:T(8,128)(2,1)}, u32[]{:S(2)}) copy-start(bf16[320,5120]{1,0:T(8,128)(2,1)} %param.22) | copy-start | bytes 9830404
  288.7 33.9 %copy-start.5 = (bf16[4,320]{1,0:T(4,128)(2,1)}, bf16[4,320]{1,0:T(4,128)(2,1)S(1)}, u32[]{:S(2)}) copy-start(bf16[4,320]{1,0:T(4,128)(2,1)S(1)} %add_convert_fusion) | copy-start | bytes 7684
Sparse Core Ops, SparseCore 0:
  37.7 36.7 all-gather.7
  115.8 61.6 reduce-scatter.6
  226.2 61.4 reduce-scatter.8
where the time goes:
time: 332 us; the launch traced here: 329 us
  waiting for transfers between devices  123 us (37%)
  blocking collectives  110 us (33%)
  matrix products  38.6 us (12%)
  local copies, waits for them, and re-layouts  26.9 us (8%)
  other arithmetic  15.8 us (5%)
  between operations  13.9 us (4%)
    unnamed x5, waiting for transfers between devices  123 us
    all_gather x2, blocking collectives, spread_rows(): return lax.all_gather(shard_rows, 'blk', axis=1, tiled=True)  38.6 us
    all_gather x2, blocking collectives, combined_all(): everything = jax.tree.map(lambda part: lax.all_gather(part, axis), value)  37.9 us
    all_gather x1, blocking collectives, local(): every_row = lax.all_gather(queries, 'blk', axis=0, tiled=True)  24.4 us
    unnamed x2, matrix products  20.4 us
    dynamic_slice x15, local copies, waits for them, and re-layouts, step(): return combine(so_far, jax.tree.map(lambda part: part[k], everything))  13.4 us
    add x15, other arithmetic, merge_parts(): merged_total = total_former * scale_former + total_latter * scale_latter  11.3 us
    dot_general x1, matrix products, local(): jnp.dot(ffn_input, gate_weight, preferred_element_type=jnp.float32)  10.7 us
  transfers between devices with their start and end apart: 3, of which 2 were waited for; matrix products, arithmetic and copies ran while one was open for 2% of the time, Pallas kernels for 0%

commit v1 on v0

v1 whole, which is shorter than its diff:
```python
import functools

import jax
import jax.numpy as jnp
from jax import lax
from jax.experimental import pallas as pl
from jax.experimental.pallas import tpu as pltpu
from jax.sharding import PartitionSpec as P

HQ = 40
KVH = 8
HEAD = 128
GROUP = HQ // KVH
MESH = pl.DeviceIdType.MESH
F32 = jnp.float32
BF16 = jnp.bfloat16

ASK, MERGE, SUM_A, ROW_A, SUM_B, ROW_B, HOME = range(7)


def chunks_of(extent, unit, wanted):
    size = unit * max(1, wanted // unit)
    while extent % size:
        size -= unit
    return size


def kernel(
    n,
    home,
    length,
    queries,
    residual,
    ffn_gain,
    query_gain,
    query_bias,
    key_hbm,
    value_hbm,
    out_hbm,
    gate_hbm,
    up_hbm,
    down_hbm,
    query_hbm,
    hidden_out,
    next_out,
    keys,
    values,
    out_w,
    gate_w,
    up_w,
    down_w,
    query_w,
    asked,
    heads,
    flat,
    stats,
    merge_send,
    merge_recv,
    sum_send,
    sum_recv,
    row_send,
    row_recv,
    home_send,
    home_recv,
    wide,
    act_in,
    load_sem,
    gate_sem,
    up_sem,
    down_sem,
    send_sem,
    recv_sem,
):
    me = lax.axis_index("blk")
    seqs, feat = residual.shape
    width = queries.shape[1]
    span = keys.shape[1]
    packed = merge_send.shape[2]
    k_step = width // gate_sem.shape[0]
    n_step = width // down_sem.shape[0]

    loads = [
        pltpu.make_async_copy(src, dst, load_sem.at[i])
        for i, (src, dst) in enumerate(
            ((key_hbm, keys), (value_hbm, values), (out_hbm, out_w), (query_hbm, query_w))
        )
    ]

    def gate_load(c):
        rows = pl.ds(pl.multiple_of(c * k_step, k_step), k_step)
        return pltpu.make_async_copy(gate_hbm.at[rows, :], gate_w.at[rows, :], gate_sem.at[c])

    def up_load(c):
        rows = pl.ds(pl.multiple_of(c * k_step, k_step), k_step)
        return pltpu.make_async_copy(up_hbm.at[rows, :], up_w.at[rows, :], up_sem.at[c])

    def down_load(c):
        cols = pl.ds(pl.multiple_of(c * n_step, n_step), n_step)
        return pltpu.make_async_copy(down_hbm.at[:, cols], down_w.at[:, cols], down_sem.at[c])

    def each(low, high, action):
        def body(i, carry):
            action(i)
            return carry

        lax.fori_loop(low, high, body, 0)

    def start(phase, source, target):
        def send(off):
            peer = lax.rem(me + off, n)
            pltpu.make_async_remote_copy(
                src_ref=source(peer),
                dst_ref=target.at[me],
                send_sem=send_sem.at[phase],
                recv_sem=recv_sem.at[phase],
                device_id={"blk": peer},
                device_id_type=MESH,
            ).start()

        each(1, n, send)

    def finish(sem, phase, target):
        part = target.at[pl.ds(0, n - 1)]
        pltpu.make_async_copy(part, part, sem.at[phase]).wait()

    def arrive(phase, target):
        finish(recv_sem, phase, target)

    barrier = pltpu.get_barrier_semaphore()

    def greet(off):
        peer = lax.rem(me + off, n)
        pl.semaphore_signal(barrier, inc=1, device_id={"blk": peer}, device_id_type=MESH)

    each(1, n, greet)
    for load in loads[:3]:
        load.start()

    def both(c):
        gate_load(c).start()
        up_load(c).start()

    each(0, width // k_step, both)
    each(0, width // n_step, lambda c: down_load(c).start())
    loads[3].start()
    pl.semaphore_wait(barrier, n - 1)

    start(ASK, lambda peer: queries, asked)
    asked[me] = queries[...]
    heads[...] = jnp.zeros_like(heads)
    loads[0].wait()
    loads[1].wait()
    arrive(ASK, asked)

    pad = 8
    rows = KVH * pad
    position = me * span + lax.broadcasted_iota(jnp.int32, (rows, span), 1)
    at_row = lax.broadcasted_iota(jnp.int32, (rows, 128), 0)
    at_lane = lax.broadcasted_iota(jnp.int32, (rows, 128), 1)
    for s in range(seqs):
        line = asked[home[s]].astype(F32)
        for h in range(HQ):
            heads[s, h // GROUP, pl.ds(h % GROUP, 1), :] = line[:, h * HEAD : (h + 1) * HEAD]
        scores = jnp.concatenate(
            [
                lax.dot_general(
                    heads[s, k].astype(BF16),
                    keys[s, :, k * HEAD : (k + 1) * HEAD],
                    (((1,), (1,)), ((), ())),
                    preferred_element_type=F32,
                )
                for k in range(KVH)
            ],
            axis=0,
        ) * HEAD ** (-0.5)
        allowed = position < length[s]
        masked = jnp.where(allowed, scores, -1e30)
        peak = jnp.max(masked, axis=1, keepdims=True)
        raised = jnp.where(allowed, jnp.exp(masked - peak), 0.0)
        total = jnp.sum(raised, axis=1, keepdims=True)
        for k in range(KVH):
            mixed = jnp.dot(
                raised[k * pad : (k + 1) * pad].astype(BF16),
                values[s, :, k * HEAD : (k + 1) * HEAD],
                preferred_element_type=F32,
            )
            for g in range(GROUP):
                h = k * GROUP + g
                flat[pl.ds(s, 1), h * HEAD : (h + 1) * HEAD] = mixed[g : g + 1]
        spread = jnp.where(at_lane == at_row, peak, 0.0) + jnp.where(
            at_lane == at_row + rows, total, 0.0
        )
        stats[pl.ds(s, 1), :] = jnp.sum(spread, axis=0, keepdims=True)

    merge_send[...] = jnp.zeros_like(merge_send)
    for d in range(n):
        merge_send[d, :, 0:feat] = flat[:, d * feat : (d + 1) * feat]
        merge_send[d, :, packed - 128 : packed] = stats[...]
    start(MERGE, lambda peer: merge_send.at[peer], merge_recv)
    merge_recv[me] = merge_send[me]
    arrive(MERGE, merge_recv)

    stat = merge_recv[:, :, packed - 128 : packed]
    scale = jnp.exp(stat - jnp.max(stat, axis=0, keepdims=True))
    lane = lax.broadcasted_iota(jnp.int32, stat.shape, 2)
    first = (me * feat) // HEAD
    feature_head = (
        me * feat + lax.broadcasted_iota(jnp.int32, (n, seqs, feat), 2)
    ) // HEAD
    factor = jnp.zeros((n, seqs, feat), F32)
    for j in range((feat + HEAD - 2) // HEAD + 1):
        h = first + j
        slot = (h // GROUP) * pad + lax.rem(h, GROUP)
        own = jnp.sum(jnp.where(lane == slot, scale, 0.0), axis=2, keepdims=True)
        whole = jnp.sum(jnp.where(lane == slot + rows, stat, 0.0), axis=2, keepdims=True)
        share = own / jnp.sum(own * whole, axis=0, keepdims=True)
        factor = jnp.where(feature_head == h, share, factor)
    context = jnp.sum(merge_recv[:, :, 0:feat] * factor, axis=0).astype(BF16)

    def reduce_over(phase, buffers):
        for d in range(n):
            sum_send[buffers, d] = flat[:, d * feat : (d + 1) * feat]
        start(phase, lambda peer: sum_send.at[buffers, peer], sum_recv.at[buffers])
        sum_recv[buffers, me] = sum_send[buffers, me]
        arrive(phase, sum_recv.at[buffers])
        return jnp.sum(sum_recv[buffers], axis=0)

    def share_rows(phase, buffers, mine, gain):
        row_send[buffers] = mine
        start(phase, lambda peer: row_send.at[buffers], row_recv.at[buffers])
        row_recv[buffers, me] = mine
        arrive(phase, row_recv.at[buffers])
        for d in range(n):
            wide[:, d * feat : (d + 1) * feat] = row_recv[buffers, d].astype(F32)
        whole = wide[...]
        spread = jnp.mean(whole * whole, axis=-1, keepdims=True)
        act_in[...] = (whole * lax.rsqrt(spread + 1e-06) * gain[...]).astype(BF16)

    loads[2].wait()

    def project(c):
        cols = pl.ds(pl.multiple_of(c * n_step, n_step), n_step)
        flat[:, cols] = jnp.dot(context, out_w[:, cols], preferred_element_type=F32)

    each(0, width // n_step, project)
    carried = (residual[...].astype(F32) + reduce_over(SUM_A, 0)).astype(BF16)
    share_rows(ROW_A, 0, carried, ffn_gain)

    hidden = gate_w.shape[1]

    def expand(c, sums):
        gate_load(c).wait()
        up_load(c).wait()
        at = pl.ds(pl.multiple_of(c * k_step, k_step), k_step)
        piece = act_in[:, at]
        return (
            sums[0] + jnp.dot(piece, gate_w[at, :], preferred_element_type=F32),
            sums[1] + jnp.dot(piece, up_w[at, :], preferred_element_type=F32),
        )

    zero = jnp.zeros((seqs, hidden), F32)
    gate, up = lax.fori_loop(0, width // k_step, expand, (zero, zero))
    activated = (gate / (1.0 + jnp.exp(-gate)) * up).astype(BF16)

    def contract(c):
        down_load(c).wait()
        cols = pl.ds(pl.multiple_of(c * n_step, n_step), n_step)
        flat[:, cols] = jnp.dot(activated, down_w[:, cols], preferred_element_type=F32)

    each(0, width // n_step, contract)
    leaving = (carried.astype(F32) + reduce_over(SUM_B, 1)).astype(BF16)
    hidden_out[...] = leaving
    share_rows(ROW_B, 1, leaving, query_gain)

    loads[3].wait()

    def ask(c, total):
        at = pl.ds(pl.multiple_of(c * k_step, k_step), k_step)
        return total + jnp.dot(act_in[:, at], query_w[at, :], preferred_element_type=F32)

    fresh = lax.fori_loop(0, width // k_step, ask, jnp.zeros((seqs, feat), F32))
    fresh = (fresh + query_bias[...]).astype(BF16).astype(F32)

    def address(d):
        row = jnp.zeros((1, feat), F32)
        for s in range(seqs):
            row = row + jnp.where(home[s] == d, fresh[s : s + 1], 0.0)
        home_send[d] = row.astype(BF16)

    for d in range(n):
        address(d)
    start(HOME, lambda peer: home_send.at[peer], home_recv)
    home_recv[me] = home_send[me]
    arrive(HOME, home_recv)
    for d in range(n):
        wide[0:1, d * feat : (d + 1) * feat] = home_recv[d].astype(F32)
    next_out[...] = wide[0:1, :].astype(BF16)

    finish(send_sem, ASK, asked)
    finish(send_sem, MERGE, merge_recv)
    finish(send_sem, SUM_A, sum_recv.at[0])
    finish(send_sem, ROW_A, row_recv.at[0])
    finish(send_sem, SUM_B, sum_recv.at[1])
    finish(send_sem, ROW_B, row_recv.at[1])
    finish(send_sem, HOME, home_recv)


def local(
    n,
    queries,
    home_device,
    lengths,
    key_cache,
    value_cache,
    residual,
    out_weight,
    ffn_gain,
    gate_weight,
    up_weight,
    down_weight,
    query_gain,
    query_weight,
    query_bias,
):
    seqs, feat = residual.shape
    width = queries.shape[1]
    packed = pl.cdiv(feat, 128) * 128 + 128
    step = chunks_of(width, 128, 512)
    vmem = pl.BlockSpec(memory_space=pltpu.VMEM)
    smem = pl.BlockSpec(memory_space=pltpu.SMEM)
    left = pl.BlockSpec(memory_space=pl.ANY)
    dma = pltpu.SemaphoreType.DMA

    def like(array):
        return pltpu.VMEM(array.shape, array.dtype)

    return pl.pallas_call(
        functools.partial(kernel, n),
        out_shape=(
            jax.ShapeDtypeStruct((seqs, feat), BF16),
            jax.ShapeDtypeStruct((1, width), BF16),
        ),
        in_specs=[smem] * 2 + [vmem] * 5 + [left] * 7,
        out_specs=(vmem, vmem),
        scratch_shapes=[
            like(key_cache),
            like(value_cache),
            like(out_weight),
            like(gate_weight),
            like(up_weight),
            like(down_weight),
            like(query_weight),
            pltpu.VMEM((n, 1, width), BF16),
            pltpu.VMEM((seqs, KVH, 8, HEAD), F32),
            pltpu.VMEM((seqs, width), F32),
            pltpu.VMEM((seqs, 128), F32),
            pltpu.VMEM((n, seqs, packed), F32),
            pltpu.VMEM((n, seqs, packed), F32),
            pltpu.VMEM((2, n, seqs, feat), F32),
            pltpu.VMEM((2, n, seqs, feat), F32),
            pltpu.VMEM((2, seqs, feat), BF16),
            pltpu.VMEM((2, n, seqs, feat), BF16),
            pltpu.VMEM((n, 1, feat), BF16),
            pltpu.VMEM((n, 1, feat), BF16),
            pltpu.VMEM((seqs, width), F32),
            pltpu.VMEM((seqs, width), BF16),
            dma((4,)),
            dma((width // step,)),
            dma((width // step,)),
            dma((width // step,)),
            dma((7,)),
            dma((7,)),
        ],
        compiler_params=pltpu.CompilerParams(
            collective_id=0, has_side_effects=True, vmem_limit_bytes=67043328
        ),
        name="decode_step",
    )(
        home_device,
        lengths,
        queries,
        residual,
        ffn_gain[None, :],
        query_gain[None, :],
        query_bias[None, :],
        key_cache,
        value_cache,
        out_weight,
        gate_weight,
        up_weight,
        down_weight,
        query_weight,
    )


def solution(mesh):
    placed = (
        P(("grp", "blk"), None),
        P("grp"),
        P("grp"),
        P("grp", "blk", None),
        P("grp", "blk", None),
        P("grp", "blk"),
        P("blk", None),
        P(),
        P(None, "blk"),
        P(None, "blk"),
        P("blk", None),
        P(),
        P(None, "blk"),
        P("blk"),
    )
    return jax.shard_map(
        functools.partial(local, mesh.shape["blk"]),
        mesh=mesh,
        in_specs=placed,
        out_specs=(P("grp", "blk"), P(("grp", "blk"), None)),
        check_vma=False,
    )
```

time: 332 us -> 115 us (0.35)
  waiting for transfers between devices: 123 us -> 0 us
  blocking collectives: 110 us -> 0 us
  Pallas kernels: 0 us -> 57.7 us
  matrix products: 38.6 us -> 0 us
  local copies, waits for them, and re-layouts: 26.9 us -> 55.6 us
  other arithmetic: 15.8 us -> 0 us
  between operations: 13.9 us -> 0.64 us
    unnamed x5 -> x0, waiting for transfers between devices: 123 us -> none
    all_gather x5 -> x0, blocking collectives: 101 us -> none  [the longest x2 38.6 us: spread_rows(): return lax.all_gather(shard_rows, 'blk', axis=1, tiled=True)]
    pallas_call x0 -> x1, Pallas kernels: none -> 57.7 us  [local(): pl.pallas_call(functools.partial(kernel, n), out_shape=(jax.ShapeDtypeStr...]
    unnamed x22 -> x5, local copies, waits for them, and re-layouts: 2.23 us -> 54.4 us
    unnamed x2 -> x0, matrix products: 20.4 us -> none
    dot_general x5 -> x0, matrix products: 18.2 us -> none  [the longest x1 10.7 us: local(): jnp.dot(ffn_input, gate_weight, preferred_element_type=jnp.float32)]
    add x31 -> x0, other arithmetic: 13.7 us -> none  [the longest x15 11.3 us: merge_parts(): merged_total = total_former * scale_former + total_latter * scale_latter]
    dynamic_slice x15 -> x0, local copies, waits for them, and re-layouts: 13.4 us -> none  [step(): return combine(so_far, jax.tree.map(lambda part: part[k], everything))]
  transfers between devices with their start and end apart: 3 -> 0, of which waited for: 2 -> 0; matrix products, arithmetic and copies ran while one was open for 2% -> 0% of each run, Pallas kernels for 0% -> 0%
where the time goes in v1:
time: 115 us; the launch traced here: 114 us
  Pallas kernels  57.7 us (50%)
  local copies, waits for them, and re-layouts  55.6 us (48%)
    pallas_call x1, Pallas kernels, local(): pl.pallas_call(functools.partial(kernel, n), out_shape=(jax.ShapeDtypeStr...  57.7 us
    unnamed x5, local copies, waits for them, and re-layouts  54.4 us

profile of v1, /device:TPU:0, one launch (start us, length us, event | category | flops | bytes accessed | tf_op | source)
XLA Modules:
  0.0 114.0 jit_solution(17632258293702385298)
XLA Ops:
  0.6 1.2 %broadcast_in_dim.11.query_bias = f32[1,320]{1,0:T(1,128)} reshape(f32[320]{0:T(512)} %param.27) | data formatting | bytes 2560 | tf_op jit(solution)/shard_map/broadcast_in_dim | solution.py:385
  1.9 5.8 %copy.18.query_hbm = bf16[5120,320]{1,0:T(8,128)(2,1)} copy(bf16[5120,320]{0,1:T(8,128)(2,1)} %param.26) | data formatting | bytes 6553600 | tf_op args[12]
  7.7 23.0 %copy.16.gate_hbm = bf16[5120,1728]{1,0:T(8,128)(2,1)} copy(bf16[5120,1728]{0,1:T(8,128)(2,1)} %param.22) | data formatting | bytes 35389440 | tf_op args[8]
  30.7 22.9 %copy.17.up_hbm = bf16[5120,1728]{1,0:T(8,128)(2,1)} copy(bf16[5120,1728]{0,1:T(8,128)(2,1)} %param.23) | data formatting | bytes 35389440 | tf_op args[9]
  53.7 57.7 %decode_step.1 = (bf16[4,320]{1,0:T(4,128)(2,1)}, bf16[1,5120]{1,0:T(2,128)(2,1)}) custom-call(s32[4]{0:T(128)} %home.1, s32[4]{0:T(128)} %length.1, bf16[1,5120]{1,0:T(2,128)(2,1)} %queries.1, bf16[4,320]{1,0:T(4,128)(2,1)} %residual.1, f32[1,5120]{1,0:T(1,128)} %bitcast.2, f32[1,5120]{1,0:T(1,128)} %bitcast.3, f32[1,320]{1,0:T(1,128)} %broadcast_in_dim.11.query_bias, ...), custom_call_target="tpu_custom_call" | custom-call | tf_op jit(solution)/shard_map/decode_step/pallas_call | solution.py:337
  111.4 1.3 %copy.21 = bf16[4,320]{1,0:T(4,128)(2,1)} copy(bf16[4,320]{1,0:T(4,128)(2,1)} %get-tuple-element.4) | data formatting | bytes 5120
  112.6 1.4 %copy.22 = bf16[1,5120]{1,0:T(2,128)(2,1)} copy(bf16[1,5120]{1,0:T(2,128)(2,1)} %get-tuple-element.5) | data formatting | bytes 20480

commit v2 on v1

--- a/solution.py
+++ b/solution.py
@@ -23,6 +23,12 @@
     while extent % size:
         size -= unit
     return size
+
+
+def dot_rows(left, right):
+    return lax.dot_general(
+        left, right, (((1,), (1,)), ((), ())), preferred_element_type=F32
+    )
 
 
 def kernel(
@@ -87,12 +93,12 @@
     ]
 
     def gate_load(c):
-        rows = pl.ds(pl.multiple_of(c * k_step, k_step), k_step)
-        return pltpu.make_async_copy(gate_hbm.at[rows, :], gate_w.at[rows, :], gate_sem.at[c])
+        cols = pl.ds(pl.multiple_of(c * k_step, k_step), k_step)
+        return pltpu.make_async_copy(gate_hbm.at[:, cols], gate_w.at[:, cols], gate_sem.at[c])
 
     def up_load(c):
-        rows = pl.ds(pl.multiple_of(c * k_step, k_step), k_step)
-        return pltpu.make_async_copy(up_hbm.at[rows, :], up_w.at[rows, :], up_sem.at[c])
+        cols = pl.ds(pl.multiple_of(c * k_step, k_step), k_step)
+        return pltpu.make_async_copy(up_hbm.at[:, cols], up_w.at[:, cols], up_sem.at[c])
 
     def down_load(c):
         cols = pl.ds(pl.multiple_of(c * n_step, n_step), n_step)
@@ -163,12 +169,7 @@
             heads[s, h // GROUP, pl.ds(h % GROUP, 1), :] = line[:, h * HEAD : (h + 1) * HEAD]
         scores = jnp.concatenate(
             [
-                lax.dot_general(
-                    heads[s, k].astype(BF16),
-                    keys[s, :, k * HEAD : (k + 1) * HEAD],
-                    (((1,), (1,)), ((), ())),
-                    preferred_element_type=F32,
-                )
+                dot_rows(heads[s, k].astype(BF16), keys[s, :, k * HEAD : (k + 1) * HEAD])
                 for k in range(KVH)
             ],
             axis=0,
@@ -246,7 +247,7 @@
     carried = (residual[...].astype(F32) + reduce_over(SUM_A, 0)).astype(BF16)
     share_rows(ROW_A, 0, carried, ffn_gain)
 
-    hidden = gate_w.shape[1]
+    hidden = gate_w.shape[0]
 
     def expand(c, sums):
         gate_load(c).wait()
@@ -254,8 +255,8 @@
         at = pl.ds(pl.multiple_of(c * k_step, k_step), k_step)
         piece = act_in[:, at]
         return (
-            sums[0] + jnp.dot(piece, gate_w[at, :], preferred_element_type=F32),
-            sums[1] + jnp.dot(piece, up_w[at, :], preferred_element_type=F32),
+            sums[0] + dot_rows(piece, gate_w[:, at]),
+            sums[1] + dot_rows(piece, up_w[:, at]),
         )
 
     zero = jnp.zeros((seqs, hidden), F32)
@@ -276,7 +277,7 @@
 
     def ask(c, total):
         at = pl.ds(pl.multiple_of(c * k_step, k_step), k_step)
-        return total + jnp.dot(act_in[:, at], query_w[at, :], preferred_element_type=F32)
+        return total + dot_rows(act_in[:, at], query_w[:, at])
 
     fresh = lax.fori_loop(0, width // k_step, ask, jnp.zeros((seqs, feat), F32))
     fresh = (fresh + query_bias[...]).astype(BF16).astype(F32)
@@ -334,6 +335,9 @@
     def like(array):
         return pltpu.VMEM(array.shape, array.dtype)
 
+    def flipped(array):
+        return pltpu.VMEM(array.shape[::-1], array.dtype)
+
     return pl.pallas_call(
         functools.partial(kernel, n),
         out_shape=(
@@ -346,10 +350,10 @@
             like(key_cache),
             like(value_cache),
             like(out_weight),
-            like(gate_weight),
-            like(up_weight),
+            flipped(gate_weight),
+            flipped(up_weight),
             like(down_weight),
-            like(query_weight),
+            flipped(query_weight),
             pltpu.VMEM((n, 1, width), BF16),
             pltpu.VMEM((seqs, KVH, 8, HEAD), F32),
             pltpu.VMEM((seqs, width), F32),
@@ -386,10 +390,10 @@
         key_cache,
         value_cache,
         out_weight,
-        gate_weight,
-        up_weight,
+        gate_weight.T,
+        up_weight.T,
         down_weight,
-        query_weight,
+        query_weight.T,
     )
 
 

time: 115 us -> 67.3 us (0.59)
  local copies, waits for them, and re-layouts: 55.6 us -> 3.86 us
  Pallas kernels: 57.7 us -> 62.5 us
    unnamed x5 -> x2, local copies, waits for them, and re-layouts: 54.4 us -> 2.61 us
    pallas_call x1, Pallas kernels: 57.7 us -> 62.5 us  [local(): pl.pallas_call(functools.partial(kernel, n), out_shape=(jax.ShapeDtypeStr...]
where the time goes in v2:
time: 67.3 us; the launch traced here: 67 us
  Pallas kernels  62.5 us (93%)
  local copies, waits for them, and re-layouts  3.86 us (6%)
    pallas_call x1, Pallas kernels, local(): pl.pallas_call(functools.partial(kernel, n), out_shape=(jax.ShapeDtypeStr...  62.5 us
    unnamed x2, local copies, waits for them, and re-layouts  2.61 us

profile of v2, /device:TPU:0, one launch (start us, length us, event | category | flops | bytes accessed | tf_op | source)
XLA Modules:
  0.0 67.0 jit_solution(9435956575180022399)
XLA Ops:
  0.6 1.2 %broadcast_in_dim.11.query_bias = f32[1,320]{1,0:T(1,128)} reshape(f32[320]{0:T(512)} %param.27) | data formatting | bytes 2560 | tf_op jit(solution)/shard_map/broadcast_in_dim | solution.py:389
  1.9 62.5 %decode_step.1 = (bf16[4,320]{1,0:T(4,128)(2,1)}, bf16[1,5120]{1,0:T(2,128)(2,1)}) custom-call(s32[4]{0:T(128)} %home.1, s32[4]{0:T(128)} %length.1, bf16[1,5120]{1,0:T(2,128)(2,1)} %queries.1, bf16[4,320]{1,0:T(4,128)(2,1)} %residual.1, f32[1,5120]{1,0:T(1,128)} %bitcast.8, f32[1,5120]{1,0:T(1,128)} %bitcast.9, f32[1,320]{1,0:T(1,128)} %broadcast_in_dim.11.query_bias, ...), custom_call_target="tpu_custom_call" | custom-call | tf_op jit(solution)/shard_map/decode_step/pallas_call | solution.py:341
  64.4 1.3 %copy.18 = bf16[4,320]{1,0:T(4,128)(2,1)} copy(bf16[4,320]{1,0:T(4,128)(2,1)} %get-tuple-element.4) | data formatting | bytes 5120
  65.6 1.4 %copy.19 = bf16[1,5120]{1,0:T(2,128)(2,1)} copy(bf16[1,5120]{1,0:T(2,128)(2,1)} %get-tuple-element.5) | data formatting | bytes 20480

commit v3 on v2

--- a/solution.py
+++ b/solution.py
@@ -109,7 +109,7 @@
             action(i)
             return carry
 
-        lax.fori_loop(low, high, body, 0)
+        lax.fori_loop(low, high, body, 0, unroll=high - low <= 16)
 
     def start(phase, source, target):
         def send(off):
@@ -146,12 +146,12 @@
         gate_load(c).start()
         up_load(c).start()
 
+    pl.semaphore_wait(barrier, n - 1)
+
+    start(ASK, lambda peer: queries, asked)
     each(0, width // k_step, both)
     each(0, width // n_step, lambda c: down_load(c).start())
     loads[3].start()
-    pl.semaphore_wait(barrier, n - 1)
-
-    start(ASK, lambda peer: queries, asked)
     asked[me] = queries[...]
     heads[...] = jnp.zeros_like(heads)
     loads[0].wait()
@@ -220,11 +220,11 @@
 
     def reduce_over(phase, buffers):
         for d in range(n):
-            sum_send[buffers, d] = flat[:, d * feat : (d + 1) * feat]
+            sum_send[buffers, d] = flat[:, d * feat : (d + 1) * feat].astype(BF16)
         start(phase, lambda peer: sum_send.at[buffers, peer], sum_recv.at[buffers])
         sum_recv[buffers, me] = sum_send[buffers, me]
         arrive(phase, sum_recv.at[buffers])
-        return jnp.sum(sum_recv[buffers], axis=0)
+        return jnp.sum(sum_recv[buffers].astype(F32), axis=0)
 
     def share_rows(phase, buffers, mine, gain):
         row_send[buffers] = mine
@@ -360,8 +360,8 @@
             pltpu.VMEM((seqs, 128), F32),
             pltpu.VMEM((n, seqs, packed), F32),
             pltpu.VMEM((n, seqs, packed), F32),
-            pltpu.VMEM((2, n, seqs, feat), F32),
-            pltpu.VMEM((2, n, seqs, feat), F32),
+            pltpu.VMEM((2, n, seqs, feat), BF16),
+            pltpu.VMEM((2, n, seqs, feat), BF16),
             pltpu.VMEM((2, seqs, feat), BF16),
             pltpu.VMEM((2, n, seqs, feat), BF16),
             pltpu.VMEM((n, 1, feat), BF16),

time: 67.3 us -> 65.6 us (0.975)
  Pallas kernels: 62.5 us -> 60.8 us
    pallas_call x1, Pallas kernels: 62.5 us -> 60.8 us  [local(): pl.pallas_call(functools.partial(kernel, n), out_shape=(jax.ShapeDtypeStr...]
where the time goes in v3:
time: 65.6 us; the launch traced here: 65.3 us
  Pallas kernels  60.8 us (93%)
  local copies, waits for them, and re-layouts  3.86 us (6%)
    pallas_call x1, Pallas kernels, local(): pl.pallas_call(functools.partial(kernel, n), out_shape=(jax.ShapeDtypeStr...  60.8 us
    unnamed x2, local copies, waits for them, and re-layouts  2.61 us

profile of v3, /device:TPU:0, one launch (start us, length us, event | category | flops | bytes accessed | tf_op | source)
XLA Modules:
  0.0 65.3 jit_solution(4429501157473213159)
XLA Ops:
  0.6 1.2 %broadcast_in_dim.11.query_bias = f32[1,320]{1,0:T(1,128)} reshape(f32[320]{0:T(512)} %param.27) | data formatting | bytes 2560 | tf_op jit(solution)/shard_map/broadcast_in_dim | solution.py:389
  1.9 60.8 %decode_step.1 = (bf16[4,320]{1,0:T(4,128)(2,1)}, bf16[1,5120]{1,0:T(2,128)(2,1)}) custom-call(s32[4]{0:T(128)} %home.1, s32[4]{0:T(128)} %length.1, bf16[1,5120]{1,0:T(2,128)(2,1)} %queries.1, bf16[4,320]{1,0:T(4,128)(2,1)} %residual.1, f32[1,5120]{1,0:T(1,128)} %bitcast.8, f32[1,5120]{1,0:T(1,128)} %bitcast.9, f32[1,320]{1,0:T(1,128)} %broadcast_in_dim.11.query_bias, ...), custom_call_target="tpu_custom_call" | custom-call | tf_op jit(solution)/shard_map/decode_step/pallas_call | solution.py:341
  62.7 1.3 %copy.18 = bf16[4,320]{1,0:T(4,128)(2,1)} copy(bf16[4,320]{1,0:T(4,128)(2,1)} %get-tuple-element.4) | data formatting | bytes 5120
  63.9 1.4 %copy.19 = bf16[1,5120]{1,0:T(2,128)(2,1)} copy(bf16[1,5120]{1,0:T(2,128)(2,1)} %get-tuple-element.5) | data formatting | bytes 20480
